TPU v7x, 32 devices: a whole 2x2x4 slice. The times are simulated.
32 devices in a mesh: groups: 2 (over y), tm: 4 (over z), space: 2 (over x), chan: 2 (over core).
Axes of the slice: x: 2, y: 2, z: 4, core: 2. Of those that a mesh axis runs over, the one named last changes fastest.
Arguments:
- latents: bfloat16 [4, 8, 4, 8, 512], P('groups', 'tm', 'space', None, 'chan'), parts along dimension 0, may hold values from -60 to 60
- conv_weight: bfloat16 [3, 3, 3, 512, 512], P(None, None, None, 'tm', 'chan'), may hold values from -0.0546875 to 0.0546875
- conv_bias: float32 [512], P('chan'), may hold values from -4 to 4
- gn_gain: float32 [512], P('chan'), may hold values from 0.5 to 1.5
- gn_shift: float32 [512], P('chan'), may hold values from -3 to 3
- up_weight: bfloat16 [3, 3, 512, 512], P(None, None, None, 'chan'), may hold values from -0.09375 to 0.09375
- up_bias: float32 [512], P('chan'), may hold values from -3 to 3
Outputs:
- decoded: bfloat16 [4, 8, 8, 16, 512], P('groups', None, 'space', 'tm', 'chan'), parts along dimension 0
There are 2 independent parts, one for each index of `groups`. A program takes and returns all parts, laid end to end along the dimension named above; an argument that names none is the same for every part. Nothing has to cross between parts.
All inputs are finite; a program needn't handle non-finite values.
Results may differ from a plain program's by a relative error of at most 0.0052.
The roundings to bfloat16 on the way count: a program that leaves them out, or rounds other values in their place, can miss the bound.
Values may be sent and summed in bfloat16 or wider, within the bound.
A program may use at most 64 MiB of HBM per device.

v0:
```python
import functools

import jax
import jax.numpy as jnp
import numpy as np
from jax import lax
from jax.experimental import pallas as pl
from jax.experimental.pallas import tpu as pltpu
from jax.sharding import PartitionSpec as P

C = 512
GROUPS = 32


def from_behind(value, axis, steps):
    count = lax.axis_size(axis)
    pairs = [(source, (source + steps) % count) for source in range(count)]
    return lax.ppermute(value, axis, pairs)


def with_halo(block, sides, width):
    for axis, dim in sides:
        count = lax.axis_size(axis)
        forward = [(i, i + 1) for i in range(count - 1)]
        backward = [(target, source) for source, target in forward]
        low = lax.ppermute(
            lax.slice_in_dim(block, block.shape[dim] - width, None, axis=dim), axis, forward
        )
        high = lax.ppermute(lax.slice_in_dim(block, 0, width, axis=dim), axis, backward)
        block = jnp.concatenate([low, block, high], axis=dim)
    return block


def causal_frames(latents):
    clip_count = latents.shape[0]
    span_count = lax.axis_size("tm")
    span_index = lax.axis_index("tm")
    tail_frames = from_behind(latents, "tm", 1)
    clip_order = jnp.arange(clip_count, dtype=jnp.int32)
    opening = (span_index - clip_order) % span_count == 0
    tail_frames = jnp.where(
        opening[:, None, None, None, None], jnp.zeros_like(tail_frames), tail_frames
    )
    return jnp.concatenate([tail_frames, latents], axis=1)


def causal_conv(latents, conv_weight, conv_bias):
    framed = causal_frames(latents)
    bordered = with_halo(framed, (("space", 2),), 1)
    gathered = lax.all_gather(bordered, "chan", axis=4, tiled=True)
    padded = jnp.pad(gathered, ((0, 0), (0, 0), (0, 0), (1, 1), (0, 0)))
    initial = jnp.zeros(latents.shape[:4] + (conv_weight.shape[4],), jnp.float32)
    summed = initial + lax.conv_general_dilated(
        padded,
        lax.all_gather(conv_weight, "tm", axis=3, tiled=True),
        (1, 1, 1),
        "VALID",
        dimension_numbers=("NDHWC", "DHWIO", "NDHWC"),
        preferred_element_type=jnp.float32,
    )
    return (summed + conv_bias).astype(jnp.bfloat16)


def moments(block):
    clip_count, frame_count, row_count, col_count, chan_count = block.shape
    group_width = C // GROUPS
    grouped_values = block.astype(jnp.float32).reshape(
        clip_count, frame_count, row_count, col_count, chan_count // group_width, group_width
    )
    group_sums = jnp.sum(grouped_values, axis=(1, 2, 3, 5))
    squared_sums = jnp.sum(grouped_values * grouped_values, axis=(1, 2, 3, 5))
    group_sums, squared_sums = lax.psum((group_sums, squared_sums), ("tm", "space"))
    element_count = float(
        frame_count
        * row_count
        * col_count
        * group_width
        * lax.axis_size("tm")
        * lax.axis_size("space")
    )
    group_mean = group_sums / element_count
    group_variance = squared_sums / element_count - group_mean * group_mean
    return (group_mean, lax.rsqrt(group_variance + 1e-06))


def activate(block, group_mean, factor, gn_gain, gn_shift):
    clip_count, frame_count, row_count, col_count, chan_count = block.shape
    group_width = C // GROUPS
    grouped_values = block.astype(jnp.float32).reshape(
        clip_count, frame_count, row_count, col_count, chan_count // group_width, group_width
    )
    normed = (grouped_values - group_mean[:, None, None, None, :, None]) * factor[
        :, None, None, None, :, None
    ]
    normed = normed.reshape(block.shape) * gn_gain + gn_shift
    return jax.nn.silu(normed).astype(jnp.bfloat16)


def relayout(block):
    return lax.all_to_all(block, "tm", split_axis=3, concat_axis=1, tiled=True)


def widen(rimmed, up_weight, up_bias):
    gathered = lax.all_gather(rimmed, "chan", axis=4, tiled=True)
    widened = jnp.repeat(jnp.repeat(gathered, 2, axis=2), 2, axis=3)[:, :, 1:-1, 1:-1]
    clip_count, frame_count, tall_count, broad_count, depth_count = widened.shape
    flat = widened.reshape(clip_count * frame_count, tall_count, broad_count, depth_count)
    output = lax.conv_general_dilated(
        flat,
        up_weight,
        (1, 1),
        "VALID",
        dimension_numbers=("NHWC", "HWIO", "NHWC"),
        preferred_element_type=jnp.float32,
    )
    output = output + up_bias
    return output.reshape(
        clip_count, frame_count, tall_count - 2, broad_count - 2, up_weight.shape[3]
    ).astype(jnp.bfloat16)


def on_device(latents, conv_weight, conv_bias, gn_gain, gn_shift, up_weight, up_bias):
    conved = causal_conv(latents, conv_weight, conv_bias)
    tiled = relayout(conved)
    group_mean, factor = moments(tiled)
    active = activate(tiled, group_mean, factor, gn_gain, gn_shift)
    rimmed = with_halo(active, (("tm", 3), ("space", 2)), 1)
    return widen(rimmed, up_weight, up_bias)


MESH = pl.DeviceIdType.MESH
SEND = jnp.bfloat16


def gather_matrix(clips, spans, per, cols):
    frames = spans * per
    pick = np.zeros((3, 3, cols, clips, frames, spans, clips, per, cols), np.float32)
    for a in range(3):
        for e in range(3):
            for j in range(cols):
                for c in range(clips):
                    for k in range(frames):
                        early, col = k - 2 + a, j - 1 + e
                        if early < 0 or not 0 <= col < cols:
                            continue
                        slot = (early + c * per) % frames
                        pick[a, e, j, c, (k + c * per) % frames, slot // per, c, slot % per, col] = 1.0
    return pick.reshape(9, cols * clips * frames, spans * clips * per * cols)


def fused(sizes, x_ref, pick_hbm, bias_hbm, gain_hbm, shift_hbm, upb_hbm, w_hbm, up_hbm, out_ref,
          pick_ref, vecs, wv, upv, rx, kept, sb, rb, halo, act, st, par, lsem, s1, r1, s2, r2, s3, r3, s4, r4, s5, r5):
    T, R, TC, CL, FR = sizes
    g, t, s, c = (lax.axis_index(n) for n in ("groups", "tm", "space", "chan"))
    cin = rx.shape[-1]
    Q = x_ref.shape[-1] // cin
    other = 1 - s
    wcopy = pltpu.make_async_copy(w_hbm, wv, lsem.at[0])
    upcopy = pltpu.make_async_copy(up_hbm, upv, lsem.at[1])
    pcopy = pltpu.make_async_copy(pick_hbm, pick_ref, lsem.at[2])
    vcopies = [
        pltpu.make_async_copy(ref, vecs.at[k], lsem.at[3 + k])
        for k, ref in enumerate((bias_hbm, gain_hbm, shift_hbm, upb_hbm))
    ]
    barrier = pltpu.get_barrier_semaphore()
    for dt in range(T):
        for ds in range(2):
            for dc in range(2):
                if dt or ds or dc:
                    pl.semaphore_signal(
                        barrier, inc=1,
                        device_id=(g, lax.rem(t + dt, T), lax.rem(s + ds, 2), lax.rem(c + dc, 2)),
                        device_id_type=MESH,
                    )
    pcopy.start()
    wcopy.start()
    for copy in vcopies:
        copy.start()
    edge = s * (R + 1)
    rx[:, :, :, pl.ds(edge, 1)] = jnp.zeros(rx.shape[:3] + (1,) + rx.shape[4:], rx.dtype)
    pl.semaphore_wait(barrier, 4 * T - 1)

    sends = []
    for q in range(Q):
        lanes = pl.ds(q * cin, cin)
        target = c * Q + q
        for dc in range(2):
            to_core = lax.rem(c + dc, 2)
            near = pltpu.make_async_remote_copy(
                src_ref=x_ref.at[:, :, :, :, lanes], dst_ref=rx.at[t, :, :, pl.ds(1, R)],
                send_sem=s1.at[q, dc, 0], recv_sem=r1.at[0, t],
                device_id=(g, target, s, to_core), device_id_type=MESH)
            far = pltpu.make_async_remote_copy(
                src_ref=x_ref.at[:, :, pl.ds((1 - s) * (R - 1), 1), :, lanes],
                dst_ref=rx.at[t, :, :, pl.ds((1 - other) * (R + 1), 1)],
                send_sem=s1.at[q, dc, 1], recv_sem=r1.at[1, t],
                device_id=(g, target, other, to_core), device_id_type=MESH)
            far.start()
            sends.append((far, None))
            if dc:
                near.start()
                sends.append((near, None))
            else:
                local = pltpu.make_async_copy(
                    x_ref.at[:, :, :, :, lanes], rx.at[t, :, :, pl.ds(1, R)], r1.at[0, t])
                pl.when(target == t)(local.start)
                pl.when(target != t)(near.start)
                sends.append((near, target != t))
    upcopy.start()
    for k, ref in enumerate((gain_hbm, shift_hbm)):
        copy = pltpu.make_async_remote_copy(
            src_ref=ref, dst_ref=par.at[k], send_sem=s5.at[k], recv_sem=r5.at[k],
            device_id=(g, t, s, 1 - c), device_id_type=MESH)
        copy.start()
        sends.append((copy, None))
    pcopy.wait()
    wcopy.wait()
    for copy in vcopies:
        copy.wait()
    for source in range(T):
        for kind, rows in ((0, pl.ds(1, R)), (1, pl.ds((1 - s) * (R + 1), 1))):
            dst = rx.at[source, :, :, rows]
            pltpu.make_async_copy(dst, dst, r1.at[kind, source]).wait()

    stacked = jnp.concatenate([rx[:, :, :, r].reshape(-1, cin) for r in range(R + 2)], axis=1)
    taken = []
    for a in range(3):
        for e in range(3):
            picked = jnp.dot(pick_ref[a * 3 + e], stacked, preferred_element_type=jnp.float32)
            taken.append((picked.astype(jnp.bfloat16), wv[a, :, e].reshape(3 * cin, wv.shape[4])))
    tile = TC * CL * FR
    for r in range(R):
        total = None
        for picked, taps in taken:
            term = jnp.dot(picked[:, r * cin:(r + 3) * cin], taps, preferred_element_type=jnp.float32)
            total = term if total is None else total + term
        kept[r] = total
        rows = pl.ds(r * tile, tile)
        for k in range(T):
            sb[k, r * tile:(r + 1) * tile, :] = total[k * tile:(k + 1) * tile].astype(sb.dtype)
        for dt in (2, 3, 1):
            to = lax.rem(t + dt, T)
            copy = pltpu.make_async_remote_copy(
                src_ref=sb.at[to, rows], dst_ref=rb.at[t, rows], send_sem=s2.at[dt, r], recv_sem=r2.at[t, r],
                device_id=(g, to, s, c), device_id_type=MESH)
            copy.start()
            sends.append((copy, None))
    parts = []
    for r in range(R):
        rows = pl.ds(r * tile, tile)
        summed = kept[r, pl.ds(pl.multiple_of(t * tile, tile), tile)]
        for dt in (1, 3, 2):
            source = lax.rem(t + dt, T)
            pltpu.make_async_copy(rb.at[source, rows], rb.at[source, rows], r2.at[source, r]).wait()
            summed = summed + rb[source, r * tile:(r + 1) * tile].astype(jnp.float32)
        parts.append(summed)
    summed = jnp.concatenate(parts, axis=0)
    conved = (summed + vecs[0]).astype(jnp.bfloat16)
    CO = conved.shape[1]
    frames = CL * FR
    halo[c, 1:R + 1, 1:TC + 1] = conved.reshape(R, TC, frames, CO)

    rims = []
    for dt in (0, -1, 1):
        for ds in range(2):
            for dc in range(2):
                if not (dt or ds or dc):
                    continue
                rows_src = pl.ds(1, R) if ds == 0 else pl.ds(1 + (1 - s) * (R - 1), 1)
                rows_dst = pl.ds(1, R) if ds == 0 else pl.ds((1 - other) * (R + 1), 1)
                rows_in = pl.ds(1, R) if ds == 0 else pl.ds((1 - s) * (R + 1), 1)
                cols_src = pl.ds(1, TC) if dt == 0 else pl.ds(TC if dt == 1 else 1, 1)
                cols_dst = pl.ds(1, TC) if dt == 0 else pl.ds(0 if dt == 1 else TC + 1, 1)
                core = lax.rem(c + dc, 2)
                copy = pltpu.make_async_remote_copy(
                    src_ref=halo.at[c, rows_src, cols_src], dst_ref=halo.at[c, rows_dst, cols_dst],
                    send_sem=s3.at[dt + 1, ds, dc], recv_sem=r3.at[dt + 1, ds, dc],
                    device_id=(g, jnp.clip(t + dt, 0, T - 1) if dt else t, s if ds == 0 else other, core),
                    device_id_type=MESH)
                there = None if dt == 0 else (t < T - 1 if dt == 1 else t > 0)
                came = None if dt == 0 else (t > 0 if dt == 1 else t < T - 1)
                landed = halo.at[core, rows_in, cols_dst]
                arrival = pltpu.make_async_copy(landed, landed, r3.at[dt + 1, ds, dc])
                rims.append((copy, there, arrival, came))

    values = conved.astype(jnp.float32).reshape(R * TC, CL, FR, CO)
    firsts = jnp.sum(jnp.sum(values, axis=0), axis=1)
    seconds = jnp.sum(jnp.sum(values * values, axis=0), axis=1)
    stats = jnp.concatenate([firsts, seconds], axis=0)
    width = C // GROUPS
    local = CO // width
    fold = (lax.broadcasted_iota(jnp.int32, (CO, 128), 0) // width
            == lax.broadcasted_iota(jnp.int32, (CO, 128), 1) % local).astype(jnp.float32)
    spread = (lax.broadcasted_iota(jnp.int32, (128, CO), 1) // width
              == lax.broadcasted_iota(jnp.int32, (128, CO), 0) % local).astype(jnp.float32)
    lane = lax.broadcasted_iota(jnp.int32, (2 * CL, 128), 1) // local
    kind = lax.broadcasted_iota(jnp.int32, (2 * CL, 128), 0)
    folded = jnp.dot(stats, fold, precision=lax.Precision.HIGHEST, preferred_element_type=jnp.float32)
    st[c, s * T + t] = jnp.sum(jnp.where(lane == kind, folded, 0.0), axis=0, keepdims=True)
    for dt in range(T):
        for ds in range(2):
            for dc in range(2):
                if dt or ds or dc:
                    copy = pltpu.make_async_remote_copy(
                        src_ref=st.at[c, s * T + t], dst_ref=st.at[c, s * T + t],
                        send_sem=s4.at[dt, ds, dc], recv_sem=r4.at[c, s * T + t],
                        device_id=(g, lax.rem(t + dt, T), lax.rem(s + ds, 2), lax.rem(c + dc, 2)),
                        device_id_type=MESH)
                    copy.start()
                    sends.append((copy, None))
    for copy, there, _, _ in rims:
        if there is None:
            copy.start()
        else:
            pl.when(there)(copy.start)
        sends.append((copy, there))
    for dt in range(T):
        for ds in range(2):
            for dc in range(2):
                if dt or ds or dc:
                    core = lax.rem(c + dc, 2)
                    place = lax.rem(s + ds, 2) * T + lax.rem(t + dt, T)
                    pltpu.make_async_copy(st.at[core, place], st.at[core, place], r4.at[core, place]).wait()
    for k in range(2):
        pltpu.make_async_copy(par.at[k], par.at[k], r5.at[k]).wait()
    for _, _, arrival, came in rims:
        if came is None:
            arrival.wait()
        else:
            pl.when(came)(arrival.wait)

    count = float(2 * T * R * TC * FR * width)
    row_at = lax.broadcasted_iota(jnp.int32, (R + 2, TC + 2, CL, FR, CO), 0)
    col_at = lax.broadcasted_iota(jnp.int32, (R + 2, TC + 2, CL, FR, CO), 1)
    outside = (row_at == edge) | ((col_at == 0) & (t == 0)) | ((col_at == TC + 1) & (t == T - 1))
    for core in range(2):
        sums = st[core, 0]
        for k in range(1, 2 * T):
            sums = sums + st[core, k]
        mean = sums / count
        squares = pltpu.roll(jnp.broadcast_to(mean, (8, 128)), 128 - CL * local, axis=1)[:1]
        factor = lax.rsqrt(squares - mean * mean + 1e-06)
        rows = jnp.where(kind < CL, jnp.broadcast_to(mean, kind.shape), jnp.broadcast_to(factor, kind.shape))
        both = jnp.dot(jnp.where(lane == kind % CL, rows, 0.0), spread,
                       precision=lax.Precision.HIGHEST, preferred_element_type=jnp.float32)
        here = c == core
        gain = jnp.where(here, vecs[1], par[0])
        shift = jnp.where(here, vecs[2], par[1])
        block_in = halo[core].astype(jnp.float32).reshape(R + 2, TC + 2, CL, FR, CO)
        v = (block_in - both[:CL][None, None, :, None, :]) * both[CL:][None, None, :, None, :]
        v = v * gain.reshape(1, 1, 1, 1, CO) + shift.reshape(1, 1, 1, 1, CO)
        v = jnp.where(outside, 0.0, v / (1.0 + jnp.exp(-v)))
        act[:, :, :, core * CO:(core + 1) * CO] = v.reshape(R + 2, TC + 2, frames, CO).astype(jnp.bfloat16)

    upcopy.wait()
    total = None
    for b in range(3):
        for e in range(3):
            lhs = jnp.concatenate(
                [act[(i + b + 1) // 2, (j + e + 1) // 2] for i in range(2 * R) for j in range(2 * TC)], axis=0)
            term = jnp.dot(lhs, upv[b, e], preferred_element_type=jnp.float32)
            total = term if total is None else total + term
    rounded = (total + vecs[3]).astype(jnp.bfloat16)
    out_ref[...] = rounded
    for copy, there in sends:
        if there is None:
            copy.wait_send()
        else:
            pl.when(there)(copy.wait_send)


def in_one_kernel(latents, conv_weight, conv_bias, gn_gain, gn_shift, up_weight, up_bias):
    T = lax.axis_size("tm")
    CL, per, R, W, depth = latents.shape
    cin, CO = conv_weight.shape[3:]
    TC, FR = W // T, T * per
    frames = CL * FR
    pick = jnp.asarray(gather_matrix(CL, T, per, W), jnp.bfloat16)
    rows = [v.reshape(1, CO) for v in (conv_bias, gn_gain, gn_shift, up_bias)]
    dma, vmem, anywhere = pltpu.SemaphoreType.DMA, pl.BlockSpec(memory_space=pltpu.VMEM), pl.BlockSpec(memory_space=pl.ANY)
    out = pl.pallas_call(
        functools.partial(fused, (T, R, TC, CL, FR)),
        out_shape=pltpu.VMEM((4 * R * TC * frames, CO), jnp.bfloat16),
        in_specs=[anywhere] * 8,
        out_specs=vmem,
        scratch_shapes=[
            pltpu.VMEM(pick.shape, jnp.bfloat16),
            pltpu.VMEM((4, 1, CO), jnp.float32),
            pltpu.VMEM(conv_weight.shape, jnp.bfloat16),
            pltpu.VMEM(up_weight.shape, jnp.bfloat16),
            pltpu.VMEM((T, CL, per, R + 2, W, cin), jnp.bfloat16),
            pltpu.VMEM((R, W * frames, CO), jnp.float32),
            pltpu.VMEM((T, R * TC * frames, CO), SEND),
            pltpu.VMEM((T, R * TC * frames, CO), SEND),
            pltpu.VMEM((2, R + 2, TC + 2, frames, CO), jnp.bfloat16),
            pltpu.VMEM((R + 2, TC + 2, frames, C), jnp.bfloat16),
            pltpu.VMEM((2, 2 * T, 1, 128), jnp.float32),
            pltpu.VMEM((2, 1, CO), jnp.float32),
            dma((7,)),
            dma((depth // cin, 2, 2)), dma((2, T)),
            dma((T, R)), dma((T, R)),
            dma((3, 2, 2)), dma((3, 2, 2)),
            dma((T, 2, 2)), dma((2, 2 * T)),
            dma((2,)), dma((2,)),
        ],
        compiler_params=pltpu.CompilerParams(collective_id=0, has_side_effects=True),
    )(latents, pick, *rows, conv_weight, up_weight)
    return out.reshape(2 * R, 2 * TC, CL, FR, CO).transpose(2, 3, 0, 1, 4)


def chosen(*operands):
    latents, conv_weight = operands[:2]
    T = lax.axis_size("tm")
    fits = (
        lax.axis_size("space") == 2 and lax.axis_size("chan") == 2 and T % 2 == 0 and latents.shape[0] == 2
        and conv_weight.shape[3] % 128 == 0 and T * latents.shape[1] == 8 and conv_weight.shape[4] == 256 and latents.shape[3] % T == 0
    )
    return (in_one_kernel if fits else on_device)(*operands)


def solution(mesh):
    placed = (
        P("groups", "tm", "space", None, "chan"),
        P(None, None, None, "tm", "chan"),
        P("chan"),
        P("chan"),
        P("chan"),
        P(None, None, None, "chan"),
        P("chan"),
    )
    return jax.shard_map(
        chosen,
        mesh=mesh,
        in_specs=placed,
        out_specs=P("groups", None, "space", "tm", "chan"),
        check_vma=False,
    )
```

profile of v0, /device:TPU:0, one launch (start us, length us, event | category | flops | bytes accessed | tf_op | source)
XLA Modules:
  0.0 23.3 jit_solution(888196108272458406)
XLA Ops:
  0.0 22.5 %shard_map.82 = bf16[256,256]{1,0:T(8,128)(2,1)S(1)} custom-call(bf16[2,2,2,8,256]{4,3,2,1,0:T(8,128)(2,1)} %x_ref.1, bf16[9,128,128]{2,1,0:T(8,128)(2,1)} %constant.2.clone.pick_hbm, f32[1,256]{1,0:T(1,128)} %bitcast.9, f32[1,256]{1,0:T(1,128)} %bitcast.10, f32[1,256]{1,0:T(1,128)} %bitcast.11, f32[1,256]{1,0:T(1,128)} %bitcast.12, ...), custom_call_target="tpu_custom_call" | custom-call | tf_op jit(solution)/shard_map/pallas_call | solution.py:381
  22.5 0.7 %copy.11 = bf16[4,4,2,8,256]{4,1,0,3,2:T(4,128)(2,1)} copy(bf16[4,4,2,8,256]{4,3,2,1,0:T(8,128)(2,1)S(1)} %bitcast.8) | data formatting | bytes 262144 | tf_op jit(solution)/shard_map/reshape | solution.py:408
where the time goes:
time: 23.4 us; the launch traced here: 23.3 us
  Pallas kernels  22.5 us (96%)
  local copies, waits for them, and re-layouts  0.72 us (3%)
    pallas_call x1, Pallas kernels, in_one_kernel(): pl.pallas_call(functools.partial(fused, (T, R, TC, CL, FR)), out_shape=pl...  22.5 us
    reshape x1, local copies, waits for them, and re-layouts, in_one_kernel(): return out.reshape(2 * R, 2 * TC, CL, FR, CO).transpose(2, 3, 0, 1, 4)  0.72 us

commit v1 on v0

--- a/solution.py
+++ b/solution.py
@@ -134,22 +134,18 @@
 
 def gather_matrix(clips, spans, per, cols):
     frames = spans * per
-    pick = np.zeros((3, 3, cols, clips, frames, spans, clips, per, cols), np.float32)
+    pick = np.zeros((3, cols, clips, frames, spans, clips, per, cols), np.float32)
     for a in range(3):
-        for e in range(3):
-            for j in range(cols):
-                for c in range(clips):
-                    for k in range(frames):
-                        early, col = k - 2 + a, j - 1 + e
-                        if early < 0 or not 0 <= col < cols:
-                            continue
-                        slot = (early + c * per) % frames
-                        pick[a, e, j, c, (k + c * per) % frames, slot // per, c, slot % per, col] = 1.0
-    return pick.reshape(9, cols * clips * frames, spans * clips * per * cols)
+        for col in range(cols):
+            for c in range(clips):
+                for k in range(2 - a, frames):
+                    slot = (k - 2 + a + c * per) % frames
+                    pick[a, col, c, (k + c * per) % frames, slot // per, c, slot % per, col] = 1.0
+    return pick.reshape(3, cols * clips * frames, spans * clips * per * cols)
 
 
 def fused(sizes, x_ref, pick_hbm, bias_hbm, gain_hbm, shift_hbm, upb_hbm, w_hbm, up_hbm, out_ref,
-          pick_ref, vecs, wv, upv, rx, kept, sb, rb, halo, act, st, par, lsem, s1, r1, s2, r2, s3, r3, s4, r4, s5, r5):
+          pick_ref, vecs, wv, upv, rx, fr, kept, sb, rb, halo, act, st, par, lsem, s1, r1, s2, r2, s3, r3, s4, r4, s5, r5):
     T, R, TC, CL, FR = sizes
     g, t, s, c = (lax.axis_index(n) for n in ("groups", "tm", "space", "chan"))
     cin = rx.shape[-1]
@@ -178,6 +174,9 @@
         copy.start()
     edge = s * (R + 1)
     rx[:, :, :, pl.ds(edge, 1)] = jnp.zeros(rx.shape[:3] + (1,) + rx.shape[4:], rx.dtype)
+    W = fr.shape[1] - 2
+    for col in (0, W + 1):
+        fr[:, col] = jnp.zeros((3,) + fr.shape[2:], fr.dtype)
     pl.semaphore_wait(barrier, 4 * T - 1)
 
     sends = []
@@ -223,41 +222,50 @@
             pltpu.make_async_copy(dst, dst, r1.at[kind, source]).wait()
 
     stacked = jnp.concatenate([rx[:, :, :, r].reshape(-1, cin) for r in range(R + 2)], axis=1)
-    taken = []
+    frames = CL * FR
     for a in range(3):
-        for e in range(3):
-            picked = jnp.dot(pick_ref[a * 3 + e], stacked, preferred_element_type=jnp.float32)
-            taken.append((picked.astype(jnp.bfloat16), wv[a, :, e].reshape(3 * cin, wv.shape[4])))
-    tile = TC * CL * FR
-    for r in range(R):
-        total = None
-        for picked, taps in taken:
-            term = jnp.dot(picked[:, r * cin:(r + 3) * cin], taps, preferred_element_type=jnp.float32)
-            total = term if total is None else total + term
-        kept[r] = total
-        rows = pl.ds(r * tile, tile)
-        for k in range(T):
-            sb[k, r * tile:(r + 1) * tile, :] = total[k * tile:(k + 1) * tile].astype(sb.dtype)
-        for dt in (2, 3, 1):
-            to = lax.rem(t + dt, T)
-            copy = pltpu.make_async_remote_copy(
-                src_ref=sb.at[to, rows], dst_ref=rb.at[t, rows], send_sem=s2.at[dt, r], recv_sem=r2.at[t, r],
-                device_id=(g, to, s, c), device_id_type=MESH)
-            copy.start()
-            sends.append((copy, None))
-    parts = []
-    for r in range(R):
-        rows = pl.ds(r * tile, tile)
-        summed = kept[r, pl.ds(pl.multiple_of(t * tile, tile), tile)]
-        for dt in (1, 3, 2):
-            source = lax.rem(t + dt, T)
-            pltpu.make_async_copy(rb.at[source, rows], rb.at[source, rows], r2.at[source, r]).wait()
-            summed = summed + rb[source, r * tile:(r + 1) * tile].astype(jnp.float32)
-        parts.append(summed)
-    summed = jnp.concatenate(parts, axis=0)
+        picked = jnp.dot(pick_ref[a], stacked, preferred_element_type=jnp.float32)
+        fr[a, 1:W + 1] = picked.astype(fr.dtype).reshape(W, frames, stacked.shape[1])
+    taps = wv.shape[0] * wv.shape[1] * wv.shape[2]
+    half = W // 2
+
+    def send(step, u):
+        side = lax.rem(t // 2 + 1 + step, 2)
+        to = 3 * side if u == 0 else 1 + side
+        return to, pltpu.make_async_remote_copy(
+            src_ref=sb.at[to], dst_ref=rb.at[t], send_sem=s2.at[step, u], recv_sem=r2.at[t],
+            device_id=(g, to, s, c), device_id_type=MESH)
+
+    def halfway(step, carry):
+        side = lax.rem(t // 2 + 1 + step, 2)
+        lhs = jnp.concatenate([
+            jnp.concatenate([
+                fr[a, pl.ds(side * half + e, half), :, (r + b) * cin:(r + b + 1) * cin].reshape(half * frames, cin)
+                for r in range(R)], axis=0)
+            for a in range(3) for b in range(3) for e in range(3)], axis=1)
+        total = jnp.dot(lhs, wv[...].reshape(taps * cin, wv.shape[4]), preferred_element_type=jnp.float32)
+        parts = total.reshape(R, 2, TC * frames, wv.shape[4])
+        kept[...] = parts
+        for u in range(2):
+            sb[side * 2 + u] = parts[:, u].astype(sb.dtype)
+        for u in range(2):
+            to, copy = send(step, u)
+            pl.when(to != t)(copy.start)
+        return carry
+
+    lax.fori_loop(0, 2, halfway, 0)
+    for step in range(2):
+        for u in range(2):
+            to, copy = send(step, u)
+            sends.append((copy, to != t))
+    summed = kept[:, lax.rem(t, 2)]
+    for dt in (1, 3, 2):
+        source = lax.rem(t + dt, T)
+        pltpu.make_async_copy(rb.at[source], rb.at[source], r2.at[source]).wait()
+        summed = summed + rb[source].astype(jnp.float32)
+    summed = summed.reshape(R * TC * frames, wv.shape[4])
     conved = (summed + vecs[0]).astype(jnp.bfloat16)
     CO = conved.shape[1]
-    frames = CL * FR
     halo[c, 1:R + 1, 1:TC + 1] = conved.reshape(R, TC, frames, CO)
 
     rims = []
@@ -353,13 +361,21 @@
         act[:, :, :, core * CO:(core + 1) * CO] = v.reshape(R + 2, TC + 2, frames, CO).astype(jnp.bfloat16)
 
     upcopy.wait()
-    total = None
+    across = {}
     for b in range(3):
+        rows = sorted({(i + b + 1) // 2 for i in range(2 * R)})
         for e in range(3):
-            lhs = jnp.concatenate(
-                [act[(i + b + 1) // 2, (j + e + 1) // 2] for i in range(2 * R) for j in range(2 * TC)], axis=0)
+            cols = sorted({(j + e + 1) // 2 for j in range(2 * TC)})
+            lhs = jnp.concatenate([act[r, q] for r in rows for q in cols], axis=0)
             term = jnp.dot(lhs, upv[b, e], preferred_element_type=jnp.float32)
-            total = term if total is None else total + term
+            term = term.reshape(len(rows), len(cols), frames, CO)
+            for k, r in enumerate(rows):
+                for j in range(2 * TC):
+                    piece = term[k, cols.index((j + e + 1) // 2)]
+                    across[b, r, j] = piece if e == 0 else across[b, r, j] + piece
+    total = jnp.concatenate([
+        across[0, (i + 1) // 2, j] + across[1, (i + 2) // 2, j] + across[2, (i + 3) // 2, j]
+        for i in range(2 * R) for j in range(2 * TC)], axis=0)
     rounded = (total + vecs[3]).astype(jnp.bfloat16)
     out_ref[...] = rounded
     for copy, there in sends:
@@ -389,16 +405,17 @@
             pltpu.VMEM(conv_weight.shape, jnp.bfloat16),
             pltpu.VMEM(up_weight.shape, jnp.bfloat16),
             pltpu.VMEM((T, CL, per, R + 2, W, cin), jnp.bfloat16),
-            pltpu.VMEM((R, W * frames, CO), jnp.float32),
-            pltpu.VMEM((T, R * TC * frames, CO), SEND),
-            pltpu.VMEM((T, R * TC * frames, CO), SEND),
+            pltpu.VMEM((3, W + 2, frames, (R + 2) * cin), jnp.bfloat16),
+            pltpu.VMEM((R, 2, TC * frames, CO), jnp.float32),
+            pltpu.VMEM((T, R, TC * frames, CO), SEND),
+            pltpu.VMEM((T, R, TC * frames, CO), SEND),
             pltpu.VMEM((2, R + 2, TC + 2, frames, CO), jnp.bfloat16),
             pltpu.VMEM((R + 2, TC + 2, frames, C), jnp.bfloat16),
             pltpu.VMEM((2, 2 * T, 1, 128), jnp.float32),
             pltpu.VMEM((2, 1, CO), jnp.float32),
             dma((7,)),
             dma((depth // cin, 2, 2)), dma((2, T)),
-            dma((T, R)), dma((T, R)),
+            dma((2, 2)), dma((T,)),
             dma((3, 2, 2)), dma((3, 2, 2)),
             dma((T, 2, 2)), dma((2, 2 * T)),
             dma((2,)), dma((2,)),
@@ -412,7 +429,7 @@
     latents, conv_weight = operands[:2]
     T = lax.axis_size("tm")
     fits = (
-        lax.axis_size("space") == 2 and lax.axis_size("chan") == 2 and T % 2 == 0 and latents.shape[0] == 2
+        lax.axis_size("space") == 2 and lax.axis_size("chan") == 2 and T == 4 and latents.shape[0] == 2
         and conv_weight.shape[3] % 128 == 0 and T * latents.shape[1] == 8 and conv_weight.shape[4] == 256 and latents.shape[3] % T == 0
     )
     return (in_one_kernel if fits else on_device)(*operands)

time: 23.4 us -> 22.6 us (0.966)
  Pallas kernels: 22.5 us -> 21.7 us
    pallas_call x1, Pallas kernels: 22.5 us -> 21.7 us  [in_one_kernel(): pl.pallas_call(functools.partial(fused, (T, R, TC, CL, FR)), out_shape=pl...]
where the time goes in v1:
time: 22.6 us; the launch traced here: 22.4 us
  Pallas kernels  21.7 us (96%)
  local copies, waits for them, and re-layouts  0.72 us (3%)
    pallas_call x1, Pallas kernels, in_one_kernel(): pl.pallas_call(functools.partial(fused, (T, R, TC, CL, FR)), out_shape=pl...  21.7 us
    reshape x1, local copies, waits for them, and re-layouts, in_one_kernel(): return out.reshape(2 * R, 2 * TC, CL, FR, CO).transpose(2, 3, 0, 1, 4)  0.72 us

profile of v1, /device:TPU:0, one launch (start us, length us, event | category | flops | bytes accessed | tf_op | source)
XLA Modules:
  0.0 22.4 jit_solution(18228953495598658089)
XLA Ops:
  0.0 21.7 %shard_map.82 = bf16[256,256]{1,0:T(8,128)(2,1)S(1)} custom-call(bf16[2,2,2,8,256]{4,3,2,1,0:T(8,128)(2,1)} %x_ref.1, bf16[3,128,128]{2,1,0:T(8,128)(2,1)} %constant.2.clone.pick_hbm, f32[1,256]{1,0:T(1,128)} %bitcast.9, f32[1,256]{1,0:T(1,128)} %bitcast.10, f32[1,256]{1,0:T(1,128)} %bitcast.11, f32[1,256]{1,0:T(1,128)} %bitcast.12, ...), custom_call_target="tpu_custom_call" | custom-call | tf_op jit(solution)/shard_map/pallas_call | solution.py:397
  21.7 0.7 %copy.11 = bf16[4,4,2,8,256]{4,1,0,3,2:T(4,128)(2,1)} copy(bf16[4,4,2,8,256]{4,3,2,1,0:T(8,128)(2,1)S(1)} %bitcast.8) | data formatting | bytes 262144 | tf_op jit(solution)/shard_map/reshape | solution.py:425

commit v2 on v1

--- a/solution.py
+++ b/solution.py
@@ -142,6 +142,14 @@
                     slot = (k - 2 + a + c * per) % frames
                     pick[a, col, c, (k + c * per) % frames, slot // per, c, slot % per, col] = 1.0
     return pick.reshape(3, cols * clips * frames, spans * clips * per * cols)
+
+
+def thirds(value):
+    high = value.astype(jnp.bfloat16)
+    rest = value - high.astype(jnp.float32)
+    middle = rest.astype(jnp.bfloat16)
+    low = (rest - middle.astype(jnp.float32)).astype(jnp.bfloat16)
+    return high, middle, low
 
 
 def fused(sizes, x_ref, pick_hbm, bias_hbm, gain_hbm, shift_hbm, upb_hbm, w_hbm, up_hbm, out_ref,
@@ -159,8 +167,8 @@
         for k, ref in enumerate((bias_hbm, gain_hbm, shift_hbm, upb_hbm))
     ]
     barrier = pltpu.get_barrier_semaphore()
-    for dt in range(T):
-        for ds in range(2):
+    for dt in (1, 2, 3, 0):
+        for ds in (1, 0):
             for dc in range(2):
                 if dt or ds or dc:
                     pl.semaphore_signal(
@@ -180,22 +188,24 @@
     pl.semaphore_wait(barrier, 4 * T - 1)
 
     sends = []
-    for q in range(Q):
-        lanes = pl.ds(q * cin, cin)
+    first = jnp.where(t <= 2 * c, 1, 0)
+    for turn in range(Q):
+        q = first if turn == 0 else 1 - first
+        lanes = pl.ds(pl.multiple_of(q * cin, cin), cin)
         target = c * Q + q
         for dc in range(2):
-            to_core = lax.rem(c + dc, 2)
-            near = pltpu.make_async_remote_copy(
-                src_ref=x_ref.at[:, :, :, :, lanes], dst_ref=rx.at[t, :, :, pl.ds(1, R)],
-                send_sem=s1.at[q, dc, 0], recv_sem=r1.at[0, t],
-                device_id=(g, target, s, to_core), device_id_type=MESH)
             far = pltpu.make_async_remote_copy(
                 src_ref=x_ref.at[:, :, pl.ds((1 - s) * (R - 1), 1), :, lanes],
                 dst_ref=rx.at[t, :, :, pl.ds((1 - other) * (R + 1), 1)],
-                send_sem=s1.at[q, dc, 1], recv_sem=r1.at[1, t],
-                device_id=(g, target, other, to_core), device_id_type=MESH)
+                send_sem=s1.at[turn, dc, 1], recv_sem=r1.at[1, t],
+                device_id=(g, target, other, lax.rem(c + dc, 2)), device_id_type=MESH)
             far.start()
             sends.append((far, None))
+        for dc in range(2):
+            near = pltpu.make_async_remote_copy(
+                src_ref=x_ref.at[:, :, :, :, lanes], dst_ref=rx.at[t, :, :, pl.ds(1, R)],
+                send_sem=s1.at[turn, dc, 0], recv_sem=r1.at[0, t],
+                device_id=(g, target, s, lax.rem(c + dc, 2)), device_id_type=MESH)
             if dc:
                 near.start()
                 sends.append((near, None))
@@ -298,12 +308,12 @@
     width = C // GROUPS
     local = CO // width
     fold = (lax.broadcasted_iota(jnp.int32, (CO, 128), 0) // width
-            == lax.broadcasted_iota(jnp.int32, (CO, 128), 1) % local).astype(jnp.float32)
+            == lax.broadcasted_iota(jnp.int32, (CO, 128), 1) % local).astype(jnp.float32).astype(jnp.bfloat16)
     spread = (lax.broadcasted_iota(jnp.int32, (128, CO), 1) // width
-              == lax.broadcasted_iota(jnp.int32, (128, CO), 0) % local).astype(jnp.float32)
+              == lax.broadcasted_iota(jnp.int32, (128, CO), 0) % local).astype(jnp.float32).astype(jnp.bfloat16)
     lane = lax.broadcasted_iota(jnp.int32, (2 * CL, 128), 1) // local
     kind = lax.broadcasted_iota(jnp.int32, (2 * CL, 128), 0)
-    folded = jnp.dot(stats, fold, precision=lax.Precision.HIGHEST, preferred_element_type=jnp.float32)
+    folded = sum(jnp.dot(part, fold, preferred_element_type=jnp.float32) for part in thirds(stats))
     st[c, s * T + t] = jnp.sum(jnp.where(lane == kind, folded, 0.0), axis=0, keepdims=True)
     for dt in range(T):
         for ds in range(2):
@@ -322,6 +332,12 @@
         else:
             pl.when(there)(copy.start)
         sends.append((copy, there))
+    for copy, there in sends:
+        if there is None:
+            copy.wait_send()
+        else:
+            pl.when(there)(copy.wait_send)
+    upcopy.wait()
     for dt in range(T):
         for ds in range(2):
             for dc in range(2):
@@ -338,9 +354,7 @@
             pl.when(came)(arrival.wait)
 
     count = float(2 * T * R * TC * FR * width)
-    row_at = lax.broadcasted_iota(jnp.int32, (R + 2, TC + 2, CL, FR, CO), 0)
-    col_at = lax.broadcasted_iota(jnp.int32, (R + 2, TC + 2, CL, FR, CO), 1)
-    outside = (row_at == edge) | ((col_at == 0) & (t == 0)) | ((col_at == TC + 1) & (t == T - 1))
+    picks = []
     for core in range(2):
         sums = st[core, 0]
         for k in range(1, 2 * T):
@@ -349,18 +363,29 @@
         squares = pltpu.roll(jnp.broadcast_to(mean, (8, 128)), 128 - CL * local, axis=1)[:1]
         factor = lax.rsqrt(squares - mean * mean + 1e-06)
         rows = jnp.where(kind < CL, jnp.broadcast_to(mean, kind.shape), jnp.broadcast_to(factor, kind.shape))
-        both = jnp.dot(jnp.where(lane == kind % CL, rows, 0.0), spread,
-                       precision=lax.Precision.HIGHEST, preferred_element_type=jnp.float32)
+        picks.append(jnp.where(lane == kind % CL, rows, 0.0))
+    both = sum(jnp.dot(part, spread, preferred_element_type=jnp.float32)
+               for part in thirds(jnp.concatenate(picks, axis=0)))
+    for core in range(2):
         here = c == core
         gain = jnp.where(here, vecs[1], par[0])
         shift = jnp.where(here, vecs[2], par[1])
-        block_in = halo[core].astype(jnp.float32).reshape(R + 2, TC + 2, CL, FR, CO)
-        v = (block_in - both[:CL][None, None, :, None, :]) * both[CL:][None, None, :, None, :]
-        v = v * gain.reshape(1, 1, 1, 1, CO) + shift.reshape(1, 1, 1, 1, CO)
-        v = jnp.where(outside, 0.0, v / (1.0 + jnp.exp(-v)))
-        act[:, :, :, core * CO:(core + 1) * CO] = v.reshape(R + 2, TC + 2, frames, CO).astype(jnp.bfloat16)
-
-    upcopy.wait()
+        means, factors = both[2 * CL * core:2 * CL * core + CL], both[2 * CL * core + CL:2 * CL * (core + 1)]
+        scale = factors * gain * 0.5
+        offset = shift * 0.5 - means * scale
+        scale, offset = (
+            jnp.concatenate([jnp.broadcast_to(v[k:k + 1], (FR, CO)) for k in range(CL)], axis=0)
+            for v in (scale, offset))
+        for r in range(R + 2):
+            for q in range(TC + 2):
+                v = halo[core, r, q].astype(jnp.float32) * scale + offset
+                v = v + v * jnp.tanh(v)
+                keep = [s > 0] if r == 0 else [s < 1] if r == R + 1 else []
+                keep += [t > 0] if q == 0 else [t < T - 1] if q == TC + 1 else []
+                if keep:
+                    v = jnp.where(functools.reduce(jnp.logical_and, keep), v, 0.0)
+                act[r, q, :, core * CO:(core + 1) * CO] = v.astype(jnp.bfloat16)
+
     across = {}
     for b in range(3):
         rows = sorted({(i + b + 1) // 2 for i in range(2 * R)})
@@ -378,11 +403,6 @@
         for i in range(2 * R) for j in range(2 * TC)], axis=0)
     rounded = (total + vecs[3]).astype(jnp.bfloat16)
     out_ref[...] = rounded
-    for copy, there in sends:
-        if there is None:
-            copy.wait_send()
-        else:
-            pl.when(there)(copy.wait_send)
 
 
 def in_one_kernel(latents, conv_weight, conv_bias, gn_gain, gn_shift, up_weight, up_bias):

time: 22.6 us -> 22.1 us (0.978)
  Pallas kernels: 21.7 us -> 21.3 us
    pallas_call x1, Pallas kernels: 21.7 us -> 21.3 us  [in_one_kernel(): pl.pallas_call(functools.partial(fused, (T, R, TC, CL, FR)), out_shape=pl...]
where the time goes in v2:
time: 22.1 us; the launch traced here: 22 us
  Pallas kernels  21.3 us (96%)
  local copies, waits for them, and re-layouts  0.72 us (3%)
    pallas_call x1, Pallas kernels, in_one_kernel(): pl.pallas_call(functools.partial(fused, (T, R, TC, CL, FR)), out_shape=pl...  21.3 us
    reshape x1, local copies, waits for them, and re-layouts, in_one_kernel(): return out.reshape(2 * R, 2 * TC, CL, FR, CO).transpose(2, 3, 0, 1, 4)  0.72 us

profile of v2, /device:TPU:0, one launch (start us, length us, event | category | flops | bytes accessed | tf_op | source)
XLA Modules:
  0.0 22.0 jit_solution(11446084717009746118)
XLA Ops:
  0.0 21.3 %shard_map.82 = bf16[256,256]{1,0:T(8,128)(2,1)S(1)} custom-call(bf16[2,2,2,8,256]{4,3,2,1,0:T(8,128)(2,1)} %x_ref.1, bf16[3,128,128]{2,1,0:T(8,128)(2,1)} %constant.2.clone.pick_hbm, f32[1,256]{1,0:T(1,128)} %bitcast.9, f32[1,256]{1,0:T(1,128)} %bitcast.10, f32[1,256]{1,0:T(1,128)} %bitcast.11, f32[1,256]{1,0:T(1,128)} %bitcast.12, ...), custom_call_target="tpu_custom_call" | custom-call | tf_op jit(solution)/shard_map/pallas_call | solution.py:417
  21.3 0.7 %copy.11 = bf16[4,4,2,8,256]{4,1,0,3,2:T(4,128)(2,1)} copy(bf16[4,4,2,8,256]{4,3,2,1,0:T(8,128)(2,1)S(1)} %bitcast.8) | data formatting | bytes 262144 | tf_op jit(solution)/shard_map/reshape | solution.py:445

commit v3 on v2

--- a/solution.py
+++ b/solution.py
@@ -152,6 +152,10 @@
     return high, middle, low
 
 
+def arrived(landed, sem):
+    pltpu.make_async_copy(landed, landed, sem).wait()
+
+
 def fused(sizes, x_ref, pick_hbm, bias_hbm, gain_hbm, shift_hbm, upb_hbm, w_hbm, up_hbm, out_ref,
           pick_ref, vecs, wv, upv, rx, fr, kept, sb, rb, halo, act, st, par, lsem, s1, r1, s2, r2, s3, r3, s4, r4, s5, r5):
     T, R, TC, CL, FR = sizes
@@ -163,7 +167,7 @@
     upcopy = pltpu.make_async_copy(up_hbm, upv, lsem.at[1])
     pcopy = pltpu.make_async_copy(pick_hbm, pick_ref, lsem.at[2])
     vcopies = [
-        pltpu.make_async_copy(ref, vecs.at[k], lsem.at[3 + k])
+        pltpu.make_async_copy(ref, vecs.at[k], lsem.at[3])
         for k, ref in enumerate((bias_hbm, gain_hbm, shift_hbm, upb_hbm))
     ]
     barrier = pltpu.get_barrier_semaphore()
@@ -187,7 +191,6 @@
         fr[:, col] = jnp.zeros((3,) + fr.shape[2:], fr.dtype)
     pl.semaphore_wait(barrier, 4 * T - 1)
 
-    sends = []
     first = jnp.where(t <= 2 * c, 1, 0)
     for turn in range(Q):
         q = first if turn == 0 else 1 - first
@@ -197,39 +200,31 @@
             far = pltpu.make_async_remote_copy(
                 src_ref=x_ref.at[:, :, pl.ds((1 - s) * (R - 1), 1), :, lanes],
                 dst_ref=rx.at[t, :, :, pl.ds((1 - other) * (R + 1), 1)],
-                send_sem=s1.at[turn, dc, 1], recv_sem=r1.at[1, t],
+                send_sem=s1.at[0], recv_sem=r1.at[0],
                 device_id=(g, target, other, lax.rem(c + dc, 2)), device_id_type=MESH)
             far.start()
-            sends.append((far, None))
         for dc in range(2):
             near = pltpu.make_async_remote_copy(
                 src_ref=x_ref.at[:, :, :, :, lanes], dst_ref=rx.at[t, :, :, pl.ds(1, R)],
-                send_sem=s1.at[turn, dc, 0], recv_sem=r1.at[0, t],
+                send_sem=s1.at[0], recv_sem=r1.at[0],
                 device_id=(g, target, s, lax.rem(c + dc, 2)), device_id_type=MESH)
             if dc:
                 near.start()
-                sends.append((near, None))
             else:
                 local = pltpu.make_async_copy(
-                    x_ref.at[:, :, :, :, lanes], rx.at[t, :, :, pl.ds(1, R)], r1.at[0, t])
+                    x_ref.at[:, :, :, :, lanes], rx.at[t, :, :, pl.ds(1, R)], r1.at[0])
                 pl.when(target == t)(local.start)
                 pl.when(target != t)(near.start)
-                sends.append((near, target != t))
     upcopy.start()
     for k, ref in enumerate((gain_hbm, shift_hbm)):
         copy = pltpu.make_async_remote_copy(
-            src_ref=ref, dst_ref=par.at[k], send_sem=s5.at[k], recv_sem=r5.at[k],
+            src_ref=ref, dst_ref=par.at[k], send_sem=s5.at[0], recv_sem=r5.at[0],
             device_id=(g, t, s, 1 - c), device_id_type=MESH)
         copy.start()
-        sends.append((copy, None))
     pcopy.wait()
     wcopy.wait()
-    for copy in vcopies:
-        copy.wait()
-    for source in range(T):
-        for kind, rows in ((0, pl.ds(1, R)), (1, pl.ds((1 - s) * (R + 1), 1))):
-            dst = rx.at[source, :, :, rows]
-            pltpu.make_async_copy(dst, dst, r1.at[kind, source]).wait()
+    arrived(vecs, lsem.at[3])
+    arrived(rx.at[:, :, :, pl.ds(1 - s, R + 1)], r1.at[0])
 
     stacked = jnp.concatenate([rx[:, :, :, r].reshape(-1, cin) for r in range(R + 2)], axis=1)
     frames = CL * FR
@@ -243,7 +238,7 @@
         side = lax.rem(t // 2 + 1 + step, 2)
         to = 3 * side if u == 0 else 1 + side
         return to, pltpu.make_async_remote_copy(
-            src_ref=sb.at[to], dst_ref=rb.at[t], send_sem=s2.at[step, u], recv_sem=r2.at[t],
+            src_ref=sb.at[to], dst_ref=rb.at[t], send_sem=s2.at[0], recv_sem=r2.at[0],
             device_id=(g, to, s, c), device_id_type=MESH)
 
     def halfway(step, carry):
@@ -264,14 +259,10 @@
         return carry
 
     lax.fori_loop(0, 2, halfway, 0)
-    for step in range(2):
-        for u in range(2):
-            to, copy = send(step, u)
-            sends.append((copy, to != t))
+    arrived(rb.at[pl.ds(0, T - 1)], r2.at[0])
     summed = kept[:, lax.rem(t, 2)]
     for dt in (1, 3, 2):
         source = lax.rem(t + dt, T)
-        pltpu.make_async_copy(rb.at[source], rb.at[source], r2.at[source]).wait()
         summed = summed + rb[source].astype(jnp.float32)
     summed = summed.reshape(R * TC * frames, wv.shape[4])
     conved = (summed + vecs[0]).astype(jnp.bfloat16)
@@ -286,20 +277,16 @@
                     continue
                 rows_src = pl.ds(1, R) if ds == 0 else pl.ds(1 + (1 - s) * (R - 1), 1)
                 rows_dst = pl.ds(1, R) if ds == 0 else pl.ds((1 - other) * (R + 1), 1)
-                rows_in = pl.ds(1, R) if ds == 0 else pl.ds((1 - s) * (R + 1), 1)
                 cols_src = pl.ds(1, TC) if dt == 0 else pl.ds(TC if dt == 1 else 1, 1)
                 cols_dst = pl.ds(1, TC) if dt == 0 else pl.ds(0 if dt == 1 else TC + 1, 1)
                 core = lax.rem(c + dc, 2)
                 copy = pltpu.make_async_remote_copy(
                     src_ref=halo.at[c, rows_src, cols_src], dst_ref=halo.at[c, rows_dst, cols_dst],
-                    send_sem=s3.at[dt + 1, ds, dc], recv_sem=r3.at[dt + 1, ds, dc],
+                    send_sem=s3.at[dt + 1], recv_sem=r3.at[dt + 1],
                     device_id=(g, jnp.clip(t + dt, 0, T - 1) if dt else t, s if ds == 0 else other, core),
                     device_id_type=MESH)
                 there = None if dt == 0 else (t < T - 1 if dt == 1 else t > 0)
-                came = None if dt == 0 else (t > 0 if dt == 1 else t < T - 1)
-                landed = halo.at[core, rows_in, cols_dst]
-                arrival = pltpu.make_async_copy(landed, landed, r3.at[dt + 1, ds, dc])
-                rims.append((copy, there, arrival, came))
+                rims.append((copy, there))
 
     values = conved.astype(jnp.float32).reshape(R * TC, CL, FR, CO)
     firsts = jnp.sum(jnp.sum(values, axis=0), axis=1)
@@ -314,51 +301,47 @@
     lane = lax.broadcasted_iota(jnp.int32, (2 * CL, 128), 1) // local
     kind = lax.broadcasted_iota(jnp.int32, (2 * CL, 128), 0)
     folded = sum(jnp.dot(part, fold, preferred_element_type=jnp.float32) for part in thirds(stats))
-    st[c, s * T + t] = jnp.sum(jnp.where(lane == kind, folded, 0.0), axis=0, keepdims=True)
+    mine = (c * 2 + s) * T + t
+    st[mine] = jnp.sum(jnp.where(lane == kind, folded, 0.0), axis=0, keepdims=True)
     for dt in range(T):
         for ds in range(2):
             for dc in range(2):
                 if dt or ds or dc:
                     copy = pltpu.make_async_remote_copy(
-                        src_ref=st.at[c, s * T + t], dst_ref=st.at[c, s * T + t],
-                        send_sem=s4.at[dt, ds, dc], recv_sem=r4.at[c, s * T + t],
+                        src_ref=st.at[mine], dst_ref=st.at[mine],
+                        send_sem=s4.at[0], recv_sem=r4.at[0],
                         device_id=(g, lax.rem(t + dt, T), lax.rem(s + ds, 2), lax.rem(c + dc, 2)),
                         device_id_type=MESH)
                     copy.start()
-                    sends.append((copy, None))
-    for copy, there, _, _ in rims:
+    for copy, there in rims:
         if there is None:
             copy.start()
         else:
             pl.when(there)(copy.start)
-        sends.append((copy, there))
-    for copy, there in sends:
-        if there is None:
-            copy.wait_send()
-        else:
-            pl.when(there)(copy.wait_send)
+    cells = R * TC + 2 * TC
+    inner, outer = halo.at[0, pl.ds(0, 2), pl.ds(0, cells // 2)], halo.at[0, pl.ds(0, 2), pl.ds(0, R + 1)]
+    local_x = c == t // 2
+    pl.when(local_x)(lambda: arrived(fr.at[0, pl.ds(0, 5)], s1.at[0]))
+    pl.when(jnp.logical_not(local_x))(lambda: arrived(fr.at[0, pl.ds(0, 6)], s1.at[0]))
+    arrived(sb.at[pl.ds(0, T - 1)], s2.at[0])
+    arrived(par, s5.at[0])
+    arrived(st.at[pl.ds(0, 4 * T - 1)], s4.at[0])
+    arrived(inner, s3.at[1])
+    pl.when(t > 0)(lambda: arrived(outer, s3.at[0]))
+    pl.when(t < T - 1)(lambda: arrived(outer, s3.at[2]))
     upcopy.wait()
-    for dt in range(T):
-        for ds in range(2):
-            for dc in range(2):
-                if dt or ds or dc:
-                    core = lax.rem(c + dc, 2)
-                    place = lax.rem(s + ds, 2) * T + lax.rem(t + dt, T)
-                    pltpu.make_async_copy(st.at[core, place], st.at[core, place], r4.at[core, place]).wait()
-    for k in range(2):
-        pltpu.make_async_copy(par.at[k], par.at[k], r5.at[k]).wait()
-    for _, _, arrival, came in rims:
-        if came is None:
-            arrival.wait()
-        else:
-            pl.when(came)(arrival.wait)
+    arrived(par, r5.at[0])
+    arrived(st.at[pl.ds(0, 4 * T - 1)], r4.at[0])
+    arrived(inner, r3.at[1])
+    pl.when(t > 0)(lambda: arrived(outer, r3.at[2]))
+    pl.when(t < T - 1)(lambda: arrived(outer, r3.at[0]))
 
     count = float(2 * T * R * TC * FR * width)
     picks = []
     for core in range(2):
-        sums = st[core, 0]
+        sums = st[core * 2 * T]
         for k in range(1, 2 * T):
-            sums = sums + st[core, k]
+            sums = sums + st[core * 2 * T + k]
         mean = sums / count
         squares = pltpu.roll(jnp.broadcast_to(mean, (8, 128)), 128 - CL * local, axis=1)[:1]
         factor = lax.rsqrt(squares - mean * mean + 1e-06)
@@ -431,14 +414,14 @@
             pltpu.VMEM((T, R, TC * frames, CO), SEND),
             pltpu.VMEM((2, R + 2, TC + 2, frames, CO), jnp.bfloat16),
             pltpu.VMEM((R + 2, TC + 2, frames, C), jnp.bfloat16),
-            pltpu.VMEM((2, 2 * T, 1, 128), jnp.float32),
+            pltpu.VMEM((4 * T, 1, 128), jnp.float32),
             pltpu.VMEM((2, 1, CO), jnp.float32),
-            dma((7,)),
-            dma((depth // cin, 2, 2)), dma((2, T)),
-            dma((2, 2)), dma((T,)),
-            dma((3, 2, 2)), dma((3, 2, 2)),
-            dma((T, 2, 2)), dma((2, 2 * T)),
-            dma((2,)), dma((2,)),
+            dma((4,)),
+            dma((1,)), dma((1,)),
+            dma((1,)), dma((1,)),
+            dma((3,)), dma((3,)),
+            dma((1,)), dma((1,)),
+            dma((1,)), dma((1,)),
         ],
         compiler_params=pltpu.CompilerParams(collective_id=0, has_side_effects=True),
     )(latents, pick, *rows, conv_weight, up_weight)
@@ -450,7 +433,8 @@
     T = lax.axis_size("tm")
     fits = (
         lax.axis_size("space") == 2 and lax.axis_size("chan") == 2 and T == 4 and latents.shape[0] == 2
-        and conv_weight.shape[3] % 128 == 0 and T * latents.shape[1] == 8 and conv_weight.shape[4] == 256 and latents.shape[3] % T == 0
+        and conv_weight.shape[3] % 128 == 0 and T * latents.shape[1] == 8 and conv_weight.shape[4] == 256 and latents.shape[2:4] == (2, 2 * T)
+        and latents.shape[1] == 2 and latents.shape[4] == 2 * conv_weight.shape[3] == 256
     )
     return (in_one_kernel if fits else on_device)(*operands)
 

time: 22.1 us -> 21.5 us (0.973)
  Pallas kernels: 21.3 us -> 20.6 us
    pallas_call x1, Pallas kernels: 21.3 us -> 20.6 us  [in_one_kernel(): pl.pallas_call(functools.partial(fused, (T, R, TC, CL, FR)), out_shape=pl...]
where the time goes in v3:
time: 21.5 us; the launch traced here: 21.3 us
  Pallas kernels  20.6 us (96%)
  local copies, waits for them, and re-layouts  0.72 us (3%)
    pallas_call x1, Pallas kernels, in_one_kernel(): pl.pallas_call(functools.partial(fused, (T, R, TC, CL, FR)), out_shape=pl...  20.6 us
    reshape x1, local copies, waits for them, and re-layouts, in_one_kernel(): return out.reshape(2 * R, 2 * TC, CL, FR, CO).transpose(2, 3, 0, 1, 4)  0.72 us

profile of v3, /device:TPU:0, one launch (start us, length us, event | category | flops | bytes accessed | tf_op | source)
XLA Modules:
  0.0 21.3 jit_solution(7016320899651727248)
XLA Ops:
  0.0 20.6 %shard_map.82 = bf16[256,256]{1,0:T(8,128)(2,1)S(1)} custom-call(bf16[2,2,2,8,256]{4,3,2,1,0:T(8,128)(2,1)} %x_ref.1, bf16[3,128,128]{2,1,0:T(8,128)(2,1)} %constant.2.clone.pick_hbm, f32[1,256]{1,0:T(1,128)} %bitcast.9, f32[1,256]{1,0:T(1,128)} %bitcast.10, f32[1,256]{1,0:T(1,128)} %bitcast.11, f32[1,256]{1,0:T(1,128)} %bitcast.12, ...), custom_call_target="tpu_custom_call" | custom-call | tf_op jit(solution)/shard_map/pallas_call | solution.py:400
  20.6 0.7 %copy.11 = bf16[4,4,2,8,256]{4,1,0,3,2:T(4,128)(2,1)} copy(bf16[4,4,2,8,256]{4,3,2,1,0:T(8,128)(2,1)S(1)} %bitcast.8) | data formatting | bytes 262144 | tf_op jit(solution)/shard_map/reshape | solution.py:428
